TPU v7x, 256 devices: a whole 4x4x8 slice. The times are simulated.
256 devices in a mesh: blk: 64 (over z_lo, x, y), grp: 4 (over z_hi, core).
Axes of the slice: x: 4, y: 4, z: 8 (z_hi: 2, z_lo: 4; z = z_hi * 4 + z_lo), core: 2. Of those that a mesh axis runs over, the one named last changes fastest.
Arguments:
- source_embed: bfloat16 [131072, 768], P(('blk', 'grp')), may hold values from -60 to 60
- target_embed: bfloat16 [8192, 768], P('blk'), may hold values from -18 to 18
- target_init: float32 [8192], P('blk'), may hold values from -6 to 6
- source_logw: float32 [131072], P(('blk', 'grp')), may hold values from -2 to 2
- target_logw: float32 [8192], P('blk'), may hold values from -2 to 2
Outputs:
- row_pot: float32 [131072], P(('blk', 'grp'))
- column_pot: float32 [8192], P('blk')
All inputs are finite; a program needn't handle non-finite values.
Results may differ from a plain program's by a relative error of at most 0.0003.
Values may be sent and summed in bfloat16 or wider, within the bound.
A program may use at most 128 MiB of HBM per device.

v0:
```python
import math
import jax
import jax.numpy as jnp
from jax import lax
from jax.sharding import PartitionSpec as P

D = 768
ITERS = 2
epsilon = 0.1
inverse_eps = 10.0


def row_update(cost_matrix, column_pot, row_logw):
    scores = (column_pot[None, :] - cost_matrix) * inverse_eps
    row_top = jnp.max(scores, axis=1)
    row_sum = jnp.sum(jnp.exp(scores - row_top[:, None]), axis=1)
    return epsilon * row_logw - epsilon * (row_top + jnp.log(row_sum))


def shards(source_embed, target_embed, target_init, source_logw, target_logw):
    factor = -1.0 / math.sqrt(D)
    init_full, logw_full = (
        lax.all_gather(target_init, "blk", axis=0, tiled=True),
        lax.all_gather(target_logw, "blk", axis=0, tiled=True),
    )
    block_index = lax.axis_index("blk")
    rows_target = target_embed.shape[0]
    cost_matrix = (
        lax.dot_general(
            source_embed,
            lax.all_gather(target_embed, "blk", axis=0, tiled=True),
            (((1,), (1,)), ((), ())),
            preferred_element_type=jnp.float32,
        )
        * factor
    )
    column_pot = init_full
    row_pot = jnp.zeros(source_logw.shape, jnp.float32)
    for iteration in range(ITERS):
        row_pot = row_update(cost_matrix, column_pot, source_logw)
        scores = (row_pot[:, None] - cost_matrix) * inverse_eps
        col_top = jnp.max(scores, axis=0)
        col_peak = lax.pmax(col_top.astype(jnp.bfloat16), ("blk", "grp")).astype(col_top.dtype)
        col_total = lax.psum(jnp.sum(jnp.exp(scores - col_peak[None, :]), axis=0), ("blk", "grp"))
        column_pot = epsilon * logw_full - epsilon * (col_peak + jnp.log(col_total))
    return (
        row_pot,
        lax.dynamic_slice_in_dim(column_pot, block_index * rows_target, rows_target, 0),
    )


def solution(mesh):
    in_specs = (P(("blk", "grp"), None), P("blk", None), P("blk"), P(("blk", "grp")), P("blk"))
    out_specs = (P(("blk", "grp")), P("blk"))
    return jax.shard_map(shards, mesh=mesh, in_specs=in_specs, out_specs=out_specs, check_vma=False)
```

profile of v0, /device:TPU:1, one launch (start us, length us, event | category | flops | bytes accessed | tf_op | source)
XLA Modules:
  0.0 764.0 jit_solution(6717112200024269160)
XLA Ops:
  7.2 0.0 copy-start
  7.2 0.0 all-gather.4.cloned.1.call-start
  7.2 0.7 all-gather.4.cloned.1.call-update
  7.9 164.8 %all-gather.1 = f32[64,1,128]{2,1,0:T(1,128)S(1)} all-gather(f32[1,1,128]{2,1,0:T(1,128)} %bitcast.10), channel_id=1, replica_groups=mesh['blk'=64,'grp'=4] {'blk'}, dimensions={0}, use_global_device_ids=true | all-gather | bytes 33280 | tf_op jit(solution)/shard_map/all_gather | solution.py:23
  172.7 155.8 %all-gather = f32[64,1,128]{2,1,0:T(1,128)S(1)} all-gather(f32[1,1,128]{2,1,0:T(1,128)} %bitcast.11), channel_id=1, replica_groups=mesh['blk'=64,'grp'=4] {'blk'}, dimensions={0}, use_global_device_ids=true | all-gather | bytes 33280 | tf_op jit(solution)/shard_map/all_gather | solution.py:24
  328.5 12.5 %all-gather.4.cloned.1.call-done = bf16[8192,768]{1,0:T(8,128)(2,1)} async-done(((bf16[128,768]{1,0:T(8,128)(2,1)}), bf16[8192,768]{1,0:T(8,128)(2,1)}) %all-gather.4.cloned.1.call-update) | async-done | bytes 12582928 | tf_op jit(solution)/shard_map/all_gather | solution.py:31
  341.0 0.0 copy-done
  341.0 14.9 %fusion = (f32[512]{0:T(512)S(1)}, f32[512,8192]{1,0:T(8,128)}) fusion(f32[8192]{0:T(1024)S(1)} %bitcast.8, bf16[512,768]{1,0:T(8,128)(2,1)S(1)} %copy-done, bf16[8192,768]{1,0:T(8,128)(2,1)} %all-gather.4.cloned.1.call-done), kind=kOutput, calls=%fused_computation.8 | convolution fusion | flops 6459227648 | bytes 30181376 | tf_op jit(solution)/shard_map/dot_general | solution.py:29
  355.9 0.0 copy-start.2
  355.9 9.3 %exponential_reduce_fusion.3 = f32[512]{0:T(512)S(1)} fusion(f32[512,8192]{1,0:T(8,128)} %get-tuple-element.3, f32[512]{0:T(512)S(1)} %get-tuple-element.2, f32[8192]{0:T(1024)S(1)} %bitcast.9), kind=kLoop, calls=%fused_computation.6 | loop fusion | flops 16776704 | bytes 16814080 | tf_op jit(solution)/shard_map/reduce_sum | solution.py:16
  365.3 0.0 copy-done.2
  365.3 8.4 %fusion.1 = bf16[8192]{0:T(1024)(128)(2,1)S(1)} fusion(f32[512,8192]{1,0:T(8,128)} %get-tuple-element.3, f32[512]{0:T(512)S(1)} %multiply_subtract_fusion.2), kind=kLoop, calls=%fused_computation.9 | loop fusion | flops 12574720 | bytes 16795648 | tf_op jit(solution)/shard_map/reduce_max | solution.py:42
  373.7 117.5 %pmax.14 = bf16[8192]{0:T(1024)(128)(2,1)S(1)} all-reduce(bf16[8192]{0:T(1024)(128)(2,1)S(1)} %fusion.1), channel_id=1, replica_groups=mesh['blk'=64,'grp'=4] {'blk','grp'}, use_global_device_ids=true, to_apply=%region_3.0 | all-reduce | flops 8192 | bytes 32768 | tf_op jit(solution)/shard_map/pmax | solution.py:43
  491.1 9.4 %exponential_reduce_fusion.2 = f32[8192]{0:T(1024)S(1)} fusion(f32[512,8192]{1,0:T(8,128)} %get-tuple-element.3, f32[8192]{0:T(1024)S(1)} %convert_element_type.13, f32[512]{0:T(512)S(1)} %multiply_subtract_fusion.2), kind=kLoop, calls=%fused_computation.4 | loop fusion | flops 16769024 | bytes 16844800 | tf_op jit(solution)/shard_map/reduce_sum | solution.py:44
  500.6 72.9 %psum.14 = f32[8192]{0:T(1024)S(1)} all-reduce(f32[8192]{0:T(1024)S(1)} %exponential_reduce_fusion.2), channel_id=1, replica_groups=mesh['blk'=64,'grp'=4] {'blk','grp'}, use_global_device_ids=true, to_apply=%region_5.0 | all-reduce | flops 8192 | bytes 65536 | tf_op jit(solution)/shard_map/psum | solution.py:44
  573.5 7.7 %fusion.2 = f32[512]{0:T(512)S(1)} fusion(f32[512,8192]{1,0:T(8,128)} %get-tuple-element.3, f32[8192]{0:T(1024)S(1)} %multiply_subtract_fusion), kind=kLoop, calls=%fused_computation.10 | loop fusion | flops 12582400 | bytes 16812032 | tf_op jit(solution)/shard_map/reduce_max | solution.py:15
  581.2 9.3 %exponential_reduce_fusion.1 = f32[512]{0:T(512)S(1)} fusion(f32[512,8192]{1,0:T(8,128)} %get-tuple-element.3, f32[512]{0:T(512)S(1)} %fusion.2, f32[8192]{0:T(1024)S(1)} %multiply_subtract_fusion), kind=kLoop, calls=%fused_computation.2 | loop fusion | flops 16776704 | bytes 16814080 | tf_op jit(solution)/shard_map/reduce_sum | solution.py:16
  590.6 0.0 copy-start.1
  590.6 8.4 %fusion.3 = bf16[8192]{0:T(1024)(128)(2,1)S(1)} fusion(f32[512,8192]{1,0:T(8,128)} %get-tuple-element.3, f32[512]{0:T(512)S(1)} %multiply_subtract_fusion.1), kind=kLoop, calls=%fused_computation.11 | loop fusion | flops 12574720 | bytes 16795648 | tf_op jit(solution)/shard_map/reduce_max | solution.py:42
  598.9 74.6 %pmax.15 = bf16[8192]{0:T(1024)(128)(2,1)S(1)} all-reduce(bf16[8192]{0:T(1024)(128)(2,1)S(1)} %fusion.3), channel_id=1, replica_groups=mesh['blk'=64,'grp'=4] {'blk','grp'}, use_global_device_ids=true, to_apply=%region_9.0 | all-reduce | flops 8192 | bytes 32768 | tf_op jit(solution)/shard_map/pmax | solution.py:43
  673.6 9.4 %exponential_reduce_fusion = f32[8192]{0:T(1024)S(1)} fusion(f32[512,8192]{1,0:T(8,128)} %get-tuple-element.3, f32[8192]{0:T(1024)S(1)} %convert_element_type.15, f32[512]{0:T(512)S(1)} %multiply_subtract_fusion.1), kind=kLoop, calls=%fused_computation | loop fusion | flops 16769024 | bytes 16844800 | tf_op jit(solution)/shard_map/reduce_sum | solution.py:44
  683.0 0.0 copy-done.1
  683.0 73.5 %psum.15 = f32[8192]{0:T(1024)S(1)} all-reduce(f32[8192]{0:T(1024)S(1)} %exponential_reduce_fusion), channel_id=1, replica_groups=mesh['blk'=64,'grp'=4] {'blk','grp'}, use_global_device_ids=true, to_apply=%region_11.0 | all-reduce | flops 8192 | bytes 65536 | tf_op jit(solution)/shard_map/psum | solution.py:44
  756.5 0.6 dynamic-slice_subtract_fusion
  (6 shorter events, 0.1 us)
Async XLA Ops:
  7.2 333.8 %copy-start = (bf16[512,768]{1,0:T(8,128)(2,1)S(1)}, bf16[512,768]{1,0:T(8,128)(2,1)}, u32[]{:S(2)}) copy-start(bf16[512,768]{1,0:T(8,128)(2,1)} %param.5) | copy-start | bytes 2359300
  7.2 333.8 %all-gather.4.cloned.1.call-start = ((), (), s32[]{:S(2)}) async-start(), calls=%async_computation | async-start | bytes 12779520 | tf_op jit(solution)/shard_map/all_gather | solution.py:31
  355.9 9.3 %copy-start.2 = (f32[512]{0:T(512)S(1)}, f32[512]{0:T(512)}, u32[]{:S(2)}) copy-start(f32[512]{0:T(512)} %param.8) | copy-start | bytes 6148
  590.6 92.5 %copy-start.1 = (f32[512]{0:T(512)}, f32[512]{0:T(512)S(1)}, u32[]{:S(2)}) copy-start(f32[512]{0:T(512)S(1)} %multiply_subtract_fusion.1) | copy-start | bytes 6148
Sparse Core Ops, SparseCore 0:
  9.8 331.1 all-gather.3
where the time goes:
time: 765 us; the launch traced here: 764 us
  blocking collectives  659 us (86%)
  other arithmetic  62.7 us (8%)
  matrix products  14.9 us (2%)
  between operations  14.1 us (2%)
  waiting for transfers between devices  13.2 us (2%)
    pmax x2, blocking collectives, shards(): lax.pmax(col_top.astype(jnp.bfloat16), ('blk', 'grp')).astype(col_top.dtype)  192 us
    all_gather x1, blocking collectives, shards(): lax.all_gather(target_init, 'blk', axis=0, tiled=True)  165 us
    all_gather x1, blocking collectives, shards(): lax.all_gather(target_logw, 'blk', axis=0, tiled=True)  156 us
    psum x2, blocking collectives, shards(): lax.psum(jnp.sum(jnp.exp(scores - col_peak[None, :]), axis=0), ('blk', 'g...  146 us
    reduce_sum x2, other arithmetic, shards(): jnp.sum(jnp.exp(scores - col_peak[None, :]), axis=0)  18.9 us
    reduce_sum x2, other arithmetic, row_update(): row_sum = jnp.sum(jnp.exp(scores - row_top[:, None]), axis=1)  18.7 us
    reduce_max x2, other arithmetic, shards(): col_top = jnp.max(scores, axis=0)  16.7 us
  transfers between devices with their start and end apart: 1, of which 1 were waited for; matrix products, arithmetic and copies ran while one was open for 0% of the time, Pallas kernels for 0%

commit v1 on v0

--- a/solution.py
+++ b/solution.py
@@ -8,6 +8,11 @@
 ITERS = 2
 epsilon = 0.1
 inverse_eps = 10.0
+
+
+def exchange_gather(x, axis, dim):
+    outgoing = jnp.stack([x] * lax.axis_size(axis))
+    return jnp.concatenate(lax.all_to_all(outgoing, axis, 0, 0), axis=dim)
 
 
 def row_update(cost_matrix, column_pot, row_logw):
@@ -21,7 +26,7 @@
     factor = -1.0 / math.sqrt(D)
     init_full, logw_full = (
         lax.all_gather(target_init, "blk", axis=0, tiled=True),
-        lax.all_gather(target_logw, "blk", axis=0, tiled=True),
+        exchange_gather(target_logw, "blk", 0),
     )
     block_index = lax.axis_index("blk")
     rows_target = target_embed.shape[0]

time: 765 us -> 765 us (level)
  blocking collectives: 659 us -> 502 us
  waiting for transfers between devices: 13.2 us -> 157 us
  starting transfers between devices: 0.04 us -> 12.6 us
    all_gather x1 -> x0, blocking collectives: 156 us -> none  [shards(): lax.all_gather(target_logw, 'blk', axis=0, tiled=True)]
    all_gather x1, waiting for transfers between devices: 12.5 us -> 156 us  [shards(): lax.all_gather(target_embed, 'blk', axis=0, tiled=True)]
    all_to_all x0 -> x1, starting transfers between devices: none -> 12.5 us  [exchange_gather(): return jnp.concatenate(lax.all_to_all(outgoing, axis, 0, 0), axis=dim)]
  transfers between devices with their start and end apart: 1 -> 2, of which waited for: 1 -> 1; matrix products, arithmetic and copies ran while one was open for 0% -> 0% of each run, Pallas kernels for 0% -> 0%
where the time goes in v1:
time: 765 us; the launch traced here: 764 us
  blocking collectives  502 us (66%)
  waiting for transfers between devices  157 us (21%)
  other arithmetic  62.5 us (8%)
  matrix products  14.9 us (2%)
  between operations  14.1 us (2%)
  starting transfers between devices  12.6 us (2%)
    pmax x2, blocking collectives, shards(): lax.pmax(col_top.astype(jnp.bfloat16), ('blk', 'grp')).astype(col_top.dtype)  192 us
    all_gather x1, blocking collectives, shards(): lax.all_gather(target_init, 'blk', axis=0, tiled=True)  163 us
    all_gather x1, waiting for transfers between devices, shards(): lax.all_gather(target_embed, 'blk', axis=0, tiled=True)  156 us
    psum x2, blocking collectives, shards(): lax.psum(jnp.sum(jnp.exp(scores - col_peak[None, :]), axis=0), ('blk', 'g...  146 us
    reduce_sum x2, other arithmetic, shards(): jnp.sum(jnp.exp(scores - col_peak[None, :]), axis=0)  18.9 us
    reduce_sum x2, other arithmetic, row_update(): row_sum = jnp.sum(jnp.exp(scores - row_top[:, None]), axis=1)  18.5 us
    reduce_max x2, other arithmetic, shards(): col_top = jnp.max(scores, axis=0)  16.7 us
  transfers between devices with their start and end apart: 2, of which 1 were waited for; matrix products, arithmetic and copies ran while one was open for 0% of the time, Pallas kernels for 0%

profile of v1, /device:TPU:1, one launch (start us, length us, event | category | flops | bytes accessed | tf_op | source)
XLA Modules:
  0.0 763.8 jit_solution(5612828132549494760)
XLA Ops:
  7.2 0.0 copy-start
  7.2 0.0 all-gather.3.cloned.1.call-start
  7.2 0.7 all-gather.3.cloned.1.call-update
  7.9 1.3 stack.2
  9.2 12.5 %all-to-all-start = ((f32[64,1,128]{2,1,0:T(1,128)}), f32[64,1,128]{2,1,0:T(1,128)S(1)}, u32[]{:S(2)}, u32[]{:S(2)}) async-start(f32[64,1,128]{2,1,0:T(1,128)} %stack.2), calls=%async_computation | async-start | bytes 65536 | tf_op jit(solution)/shard_map/all_to_all | solution.py:15
  21.7 163.2 %all-gather = f32[64,1,128]{2,1,0:T(1,128)S(1)} all-gather(f32[1,1,128]{2,1,0:T(1,128)} %bitcast.9), channel_id=1, replica_groups=mesh['blk'=64,'grp'=4] {'blk'}, dimensions={0}, use_global_device_ids=true | all-gather | bytes 33280 | tf_op jit(solution)/shard_map/all_gather | solution.py:28
  184.9 0.0 all-to-all-done
  185.0 156.0 %all-gather.3.cloned.1.call-done = bf16[8192,768]{1,0:T(8,128)(2,1)} async-done(((bf16[128,768]{1,0:T(8,128)(2,1)}), bf16[8192,768]{1,0:T(8,128)(2,1)}) %all-gather.3.cloned.1.call-update) | async-done | bytes 12582928 | tf_op jit(solution)/shard_map/all_gather | solution.py:36
  341.0 0.0 copy-done
  341.0 14.9 %fusion = (f32[512]{0:T(512)S(1)}, f32[512,8192]{1,0:T(8,128)}) fusion(f32[8192]{0:T(1024)S(1)} %bitcast.7, bf16[512,768]{1,0:T(8,128)(2,1)S(1)} %copy-done, bf16[8192,768]{1,0:T(8,128)(2,1)} %all-gather.3.cloned.1.call-done), kind=kOutput, calls=%fused_computation.8 | convolution fusion | flops 6459227648 | bytes 30181376 | tf_op jit(solution)/shard_map/dot_general | solution.py:34
  356.0 9.2 %exponential_reduce_fusion.3 = f32[512]{0:T(512)S(1)} fusion(f32[512,8192]{1,0:T(8,128)} %get-tuple-element.3, f32[512]{0:T(512)S(1)} %get-tuple-element.2, f32[8192]{0:T(1024)S(1)} %bitcast.8), kind=kLoop, calls=%fused_computation.6 | loop fusion | flops 16776704 | bytes 16814080 | tf_op jit(solution)/shard_map/reduce_sum | solution.py:21
  365.1 0.0 copy-done.2
  365.1 8.4 %fusion.1 = bf16[8192]{0:T(1024)(128)(2,1)S(1)} fusion(f32[512,8192]{1,0:T(8,128)} %get-tuple-element.3, f32[512]{0:T(512)S(1)} %multiply_subtract_fusion.2), kind=kLoop, calls=%fused_computation.9 | loop fusion | flops 12574720 | bytes 16795648 | tf_op jit(solution)/shard_map/reduce_max | solution.py:47
  373.5 118.4 %pmax.14 = bf16[8192]{0:T(1024)(128)(2,1)S(1)} all-reduce(bf16[8192]{0:T(1024)(128)(2,1)S(1)} %fusion.1), channel_id=1, replica_groups=mesh['blk'=64,'grp'=4] {'blk','grp'}, use_global_device_ids=true, to_apply=%region_3.0 | all-reduce | flops 8192 | bytes 32768 | tf_op jit(solution)/shard_map/pmax | solution.py:48
  491.9 9.4 %exponential_reduce_fusion.2 = f32[8192]{0:T(1024)S(1)} fusion(f32[512,8192]{1,0:T(8,128)} %get-tuple-element.3, f32[8192]{0:T(1024)S(1)} %convert_element_type.13, f32[512]{0:T(512)S(1)} %multiply_subtract_fusion.2), kind=kLoop, calls=%fused_computation.4 | loop fusion | flops 16769024 | bytes 16844800 | tf_op jit(solution)/shard_map/reduce_sum | solution.py:49
  501.4 72.7 %psum.14 = f32[8192]{0:T(1024)S(1)} all-reduce(f32[8192]{0:T(1024)S(1)} %exponential_reduce_fusion.2), channel_id=1, replica_groups=mesh['blk'=64,'grp'=4] {'blk','grp'}, use_global_device_ids=true, to_apply=%region_5.0 | all-reduce | flops 8192 | bytes 65536 | tf_op jit(solution)/shard_map/psum | solution.py:49
  574.1 7.7 %fusion.2 = f32[512]{0:T(512)S(1)} fusion(f32[512,8192]{1,0:T(8,128)} %get-tuple-element.3, f32[8192]{0:T(1024)S(1)} %multiply_subtract_fusion), kind=kLoop, calls=%fused_computation.10 | loop fusion | flops 12582400 | bytes 16812032 | tf_op jit(solution)/shard_map/reduce_max | solution.py:20
  581.9 9.3 %exponential_reduce_fusion.1 = f32[512]{0:T(512)S(1)} fusion(f32[512,8192]{1,0:T(8,128)} %get-tuple-element.3, f32[512]{0:T(512)S(1)} %fusion.2, f32[8192]{0:T(1024)S(1)} %multiply_subtract_fusion), kind=kLoop, calls=%fused_computation.2 | loop fusion | flops 16776704 | bytes 16814080 | tf_op jit(solution)/shard_map/reduce_sum | solution.py:21
  591.2 0.0 copy-start.1
  591.2 8.4 %fusion.3 = bf16[8192]{0:T(1024)(128)(2,1)S(1)} fusion(f32[512,8192]{1,0:T(8,128)} %get-tuple-element.3, f32[512]{0:T(512)S(1)} %multiply_subtract_fusion.1), kind=kLoop, calls=%fused_computation.11 | loop fusion | flops 12574720 | bytes 16795648 | tf_op jit(solution)/shard_map/reduce_max | solution.py:47
  599.6 74.1 %pmax.15 = bf16[8192]{0:T(1024)(128)(2,1)S(1)} all-reduce(bf16[8192]{0:T(1024)(128)(2,1)S(1)} %fusion.3), channel_id=1, replica_groups=mesh['blk'=64,'grp'=4] {'blk','grp'}, use_global_device_ids=true, to_apply=%region_9.0 | all-reduce | flops 8192 | bytes 32768 | tf_op jit(solution)/shard_map/pmax | solution.py:48
  673.6 9.4 %exponential_reduce_fusion = f32[8192]{0:T(1024)S(1)} fusion(f32[512,8192]{1,0:T(8,128)} %get-tuple-element.3, f32[8192]{0:T(1024)S(1)} %convert_element_type.15, f32[512]{0:T(512)S(1)} %multiply_subtract_fusion.1), kind=kLoop, calls=%fused_computation | loop fusion | flops 16769024 | bytes 16844800 | tf_op jit(solution)/shard_map/reduce_sum | solution.py:49
  683.1 73.3 %psum.15 = f32[8192]{0:T(1024)S(1)} all-reduce(f32[8192]{0:T(1024)S(1)} %exponential_reduce_fusion), channel_id=1, replica_groups=mesh['blk'=64,'grp'=4] {'blk','grp'}, use_global_device_ids=true, to_apply=%region_11.0 | all-reduce | flops 8192 | bytes 65536 | tf_op jit(solution)/shard_map/psum | solution.py:49
  756.4 0.6 dynamic-slice_subtract_fusion
  (8 shorter events, 0.1 us)
Async XLA Ops:
  7.2 333.9 %copy-start = (bf16[512,768]{1,0:T(8,128)(2,1)S(1)}, bf16[512,768]{1,0:T(8,128)(2,1)}, u32[]{:S(2)}) copy-start(bf16[512,768]{1,0:T(8,128)(2,1)} %param.5) | copy-start | bytes 2359300
  7.2 333.8 %all-gather.3.cloned.1.call-start = ((), (), s32[]{:S(2)}) async-start(), calls=%async_computation.1 | async-start | bytes 12779520 | tf_op jit(solution)/shard_map/all_gather | solution.py:36
  9.2 175.7 %all-to-all-start = ((f32[64,1,128]{2,1,0:T(1,128)}), f32[64,1,128]{2,1,0:T(1,128)S(1)}, u32[]{:S(2)}, u32[]{:S(2)}) async-start(f32[64,1,128]{2,1,0:T(1,128)} %stack.2), calls=%async_computation | async-start | bytes 65536 | tf_op jit(solution)/shard_map/all_to_all | solution.py:15
  356.0 9.2 %copy-start.2 = (f32[512]{0:T(512)S(1)}, f32[512]{0:T(512)}, u32[]{:S(2)}) copy-start(f32[512]{0:T(512)} %param.8) | copy-start | bytes 6148
  591.2 91.9 %copy-start.1 = (f32[512]{0:T(512)}, f32[512]{0:T(512)S(1)}, u32[]{:S(2)}) copy-start(f32[512]{0:T(512)S(1)} %multiply_subtract_fusion.1) | copy-start | bytes 6148
Sparse Core Ops, SparseCore 0:
  9.8 331.2 all-gather.2
